TPU v7x, 32 devices: a whole 2x2x4 slice. The times are simulated.
32 devices in a mesh: rep: 4 (over x, core), fsdp: 4 (over z), seq: 2 (over y).
Axes of the slice: x: 2, y: 2, z: 4, core: 2. Of those that a mesh axis runs over, the one named last changes fastest.
Arguments:
- tokens: bfloat16 [16, 592, 1024], P(('rep', 'fsdp'), 'seq'), may hold values from -6 to 6
- slot_mask: int32 [16], P(('rep', 'fsdp')), may hold values 0 or 1
- cotangent: bfloat16 [16, 592, 1024], P(('rep', 'fsdp'), 'seq'), may hold values from -6 to 6
- w_qkv: float32 [1024, 3072], P('fsdp'), may hold values from -0.25 to 0.25
- w_out: float32 [1024, 1024], P('fsdp'), may hold values from -0.75 to 0.75
- w_fc1: float32 [1024, 4096], P('fsdp'), may hold values from -0.1875 to 0.1875
- w_fc2: float32 [4096, 1024], P('fsdp'), may hold values from -0.125 to 0.125
- ln_gains: float32 [2, 1024], P(None, 'fsdp'), may hold values from 0.5 to 1.5
- biases: float32 [6, 1024], P(None, 'fsdp'), may hold values from -2 to 2
- fc1_bias: float32 [4096], P('fsdp'), may hold values from -2 to 2
Outputs:
- output: bfloat16 [16, 592, 1024], P(('rep', 'fsdp'), 'seq')
- grad_tokens: bfloat16 [16, 592, 1024], P(('rep', 'fsdp'), 'seq')
- grad_w_qkv: float32 [1024, 3072], P('fsdp')
- grad_w_out: float32 [1024, 1024], P('fsdp')
- grad_w_fc1: float32 [1024, 4096], P('fsdp')
- grad_w_fc2: float32 [4096, 1024], P('fsdp')
- grad_ln_gains: float32 [2, 1024], P(None, 'fsdp')
- grad_biases: float32 [6, 1024], P(None, 'fsdp')
- grad_fc1_bias: float32 [4096], P('fsdp')
All inputs are finite; a program needn't handle non-finite values. No bound on the sum of `slot_mask` on one device may be relied on, other than what follows from the above.
Results may differ from a plain program's by a relative error of at most 0.02.
The roundings to bfloat16 on the way count: a program that leaves them out, or rounds other values in their place, can miss the bound.
Values may be sent and summed in bfloat16 or wider, within the bound.
No kernel may reach another device: no remote copies, remote signals or barrier semaphores. Data moves between devices by JAX's collectives and lax.ppermute only.
A program may use at most 192 MiB of HBM per device.

v0:
```python
import jax
import jax.numpy as jnp
from jax import lax
from jax.sharding import PartitionSpec as P

HEADS = 16
HEAD_DIM = 64
IMG_TOK = 577
EPSILON = 1e-05
NEGATIVE = -1e30


def normalize(inputs, gain_row, shift_row):
    center = inputs - jnp.mean(inputs, axis=-1, keepdims=True)
    inverse = lax.rsqrt(jnp.mean(center * center, axis=-1, keepdims=True) + EPSILON)
    scaled = center * inverse
    return (scaled * gain_row + shift_row, scaled, inverse)


def norm_back(grad_in, scaled, inverse, gain_row):
    weighted = grad_in * gain_row
    return inverse * (
        weighted
        - jnp.mean(weighted, axis=-1, keepdims=True)
        - scaled * jnp.mean(weighted * scaled, axis=-1, keepdims=True)
    )


def across_rows(left_rows, right_rows):
    return lax.dot_general(
        left_rows, right_rows, (((0,), (0,)), ((), ())), preferred_element_type=jnp.float32
    )


def times_transposed(left_rows, right_rows):
    return lax.dot_general(
        left_rows, right_rows, (((1,), (1,)), ((), ())), preferred_element_type=jnp.float32
    )


def split_heads(matrix):
    return matrix.reshape(matrix.shape[0], HEADS, HEAD_DIM)


def masked_scores(query_rows, key_rows):
    scores = jnp.einsum(
        "qhd,khd->hqk",
        split_heads(query_rows),
        split_heads(key_rows),
        preferred_element_type=jnp.float32,
    )
    valid_keys = jnp.arange(key_rows.shape[0]) < IMG_TOK
    return jnp.where(valid_keys[None, None, :], scores, NEGATIVE)


def attend_slot(blocks_in):
    query_rows, key_rows, value_rows = blocks_in
    scores = masked_scores(query_rows, key_rows)
    highest = jnp.max(scores, axis=-1, keepdims=True)
    exponent = jnp.exp(scores - highest)
    total_sum = jnp.sum(exponent, axis=-1, keepdims=True)
    weights = (exponent / total_sum).astype(jnp.bfloat16)
    mixed_rows = jnp.einsum(
        "hqk,khd->qhd", weights, split_heads(value_rows), preferred_element_type=jnp.float32
    )
    return (mixed_rows.reshape(query_rows.shape[0], -1), highest + jnp.log(total_sum))


def attend_back(blocks_in):
    query_rows, key_rows, value_rows, log_total, grad_rows = blocks_in
    scores = masked_scores(query_rows, key_rows)
    probability = jnp.exp(scores - log_total)
    grad_heads = split_heads(grad_rows)
    grad_probs = jnp.einsum(
        "qhd,khd->hqk", grad_heads, split_heads(value_rows), preferred_element_type=jnp.float32
    )
    inner_sum = jnp.sum(probability * grad_probs, axis=-1, keepdims=True)
    grad_scores = (probability * (grad_probs - inner_sum)).astype(jnp.bfloat16)
    grad_query = jnp.einsum(
        "hqk,khd->qhd", grad_scores, split_heads(key_rows), preferred_element_type=jnp.float32
    )
    grad_key = jnp.einsum(
        "hqk,qhd->khd", grad_scores, split_heads(query_rows), preferred_element_type=jnp.float32
    )
    grad_value = jnp.einsum(
        "hqk,qhd->khd",
        probability.astype(jnp.bfloat16),
        grad_heads,
        preferred_element_type=jnp.float32,
    )
    key_count = key_rows.shape[0]
    return (
        grad_query.reshape(query_rows.shape[0], -1),
        grad_key.reshape(key_count, -1),
        grad_value.reshape(key_count, -1),
    )


def on_device(tokens, slot_mask, cotangent, w_qkv, w_out, w_fc1, w_fc2, ln_gains, biases, fc1_bias):
    slot_count, row_count, feature_width = tokens.shape
    low_qkv = w_qkv.astype(jnp.bfloat16)
    low_out = w_out.astype(jnp.bfloat16)
    low_fc1 = w_fc1.astype(jnp.bfloat16)
    low_fc2 = w_fc2.astype(jnp.bfloat16)
    low_gains = ln_gains.astype(jnp.bfloat16)
    low_biases = biases.astype(jnp.bfloat16)
    low_fc1_bias = fc1_bias.astype(jnp.bfloat16)
    gathered = (
        lax.all_gather(low_qkv, "fsdp", axis=0, tiled=True),
        lax.all_gather(low_out, "fsdp", axis=0, tiled=True),
        lax.all_gather(low_fc1, "fsdp", axis=0, tiled=True),
        lax.all_gather(low_fc2, "fsdp", axis=0, tiled=True),
        lax.all_gather(low_gains, "fsdp", axis=1, tiled=True),
        lax.all_gather(low_biases, "fsdp", axis=1, tiled=True),
        lax.all_gather(low_fc1_bias, "fsdp", axis=0, tiled=True),
    )
    big_qkv, big_out, big_fc1, big_fc2, gain_rows, bias_rows, fc1_shift = gathered
    gain_values = gain_rows.astype(jnp.float32)
    shift_values = bias_rows.astype(jnp.float32)
    hidden_shift = fc1_shift.astype(jnp.float32)
    head_scale = HEAD_DIM ** (-0.5)
    positions = lax.axis_index("seq") * row_count + jnp.arange(row_count)
    keep_mask = (
        slot_mask.astype(jnp.float32)[:, None] * (positions < IMG_TOK).astype(jnp.float32)[None, :]
    )
    keep_mask = keep_mask.reshape(-1, 1)
    inputs = tokens.astype(jnp.float32).reshape(-1, feature_width)
    normed_full, scaled_one, inverse_one = normalize(inputs, gain_values[0], shift_values[0])
    normed = normed_full.astype(jnp.bfloat16)
    joined = jnp.dot(normed, big_qkv, preferred_element_type=jnp.float32)
    queries = ((joined[:, :feature_width] + shift_values[1]) * head_scale).astype(jnp.bfloat16)
    keys_local = (
        joined[:, feature_width : 2 * feature_width]
        .astype(jnp.bfloat16)
        .reshape(slot_count, row_count, feature_width)
    )
    values_local = (
        (joined[:, 2 * feature_width :] + shift_values[2])
        .astype(jnp.bfloat16)
        .reshape(slot_count, row_count, feature_width)
    )
    slot_queries = queries.reshape(slot_count, row_count, feature_width)
    keys_all, values_all = (
        lax.all_gather(keys_local, "seq", axis=1, tiled=True),
        lax.all_gather(values_local, "seq", axis=1, tiled=True),
    )
    mixed_rows, log_total = lax.map(attend_slot, (slot_queries, keys_all, values_all))
    mixed_low = mixed_rows.reshape(-1, feature_width).astype(jnp.bfloat16)
    middle = inputs + (
        jnp.dot(mixed_low, big_out, preferred_element_type=jnp.float32) + shift_values[3]
    )
    normed_two_full, scaled_two, inverse_two = normalize(middle, gain_values[1], shift_values[4])
    normed_two = normed_two_full.astype(jnp.bfloat16)
    hidden = jnp.dot(normed_two, big_fc1, preferred_element_type=jnp.float32) + hidden_shift
    gate_values = jax.nn.sigmoid(1.702 * hidden)
    active = (hidden * gate_values).astype(jnp.bfloat16)
    result = jnp.dot(active, big_fc2, preferred_element_type=jnp.float32) + shift_values[5]
    output = ((middle + result) * keep_mask).astype(jnp.bfloat16).reshape(tokens.shape)
    again = (
        lax.all_gather(low_qkv, "fsdp", axis=0, tiled=True),
        lax.all_gather(low_out, "fsdp", axis=0, tiled=True),
        lax.all_gather(low_fc1, "fsdp", axis=0, tiled=True),
        lax.all_gather(low_fc2, "fsdp", axis=0, tiled=True),
        lax.all_gather(low_gains, "fsdp", axis=1, tiled=True),
        lax.all_gather(low_biases, "fsdp", axis=1, tiled=True),
        lax.all_gather(low_fc1_bias, "fsdp", axis=0, tiled=True),
    )
    back_qkv, back_out, back_fc1, back_fc2, back_gain_rows = (
        again[0],
        again[1],
        again[2],
        again[3],
        again[4],
    )
    back_gains = back_gain_rows.astype(jnp.float32)
    incoming = cotangent.astype(jnp.float32).reshape(-1, feature_width) * keep_mask
    grad_result = incoming.astype(jnp.bfloat16)
    grad_fc2 = across_rows(active, grad_result)
    grad_shift_five = jnp.sum(grad_result.astype(jnp.float32), axis=0)
    grad_active = times_transposed(grad_result, back_fc2)
    grad_hidden = (
        grad_active * (gate_values + 1.702 * hidden * gate_values * (1.0 - gate_values))
    ).astype(jnp.bfloat16)
    grad_fc1 = across_rows(normed_two, grad_hidden)
    grad_hidden_shift = jnp.sum(grad_hidden.astype(jnp.float32), axis=0)
    grad_normed_two = times_transposed(grad_hidden, back_fc1)
    grad_gain_two = jnp.sum(grad_normed_two * scaled_two, axis=0)
    grad_shift_four = jnp.sum(grad_normed_two, axis=0)
    grad_middle = incoming + norm_back(grad_normed_two, scaled_two, inverse_two, back_gains[1])
    grad_branch = grad_middle.astype(jnp.bfloat16)
    grad_out = across_rows(mixed_low, grad_branch)
    grad_shift_three = jnp.sum(grad_branch.astype(jnp.float32), axis=0)
    grad_mixed = times_transposed(grad_branch, back_out).astype(jnp.bfloat16)
    grad_query, key_part, value_part = lax.map(
        attend_back,
        (
            slot_queries,
            keys_all,
            values_all,
            log_total,
            grad_mixed.reshape(slot_count, row_count, feature_width),
        ),
    )
    grad_keys, grad_values = (
        lax.psum_scatter(
            key_part.astype(jnp.bfloat16), "seq", scatter_dimension=1, tiled=True
        ).astype(jnp.float32),
        lax.psum_scatter(
            value_part.astype(jnp.bfloat16), "seq", scatter_dimension=1, tiled=True
        ).astype(jnp.float32),
    )
    query_grad_low = (grad_query.astype(jnp.bfloat16) * head_scale).reshape(-1, feature_width)
    key_grad_low = grad_keys.astype(jnp.bfloat16).reshape(-1, feature_width)
    value_grad_low = grad_values.astype(jnp.bfloat16).reshape(-1, feature_width)
    grad_joined = jnp.concatenate([query_grad_low, key_grad_low, value_grad_low], axis=1)
    grad_qkv = across_rows(normed, grad_joined)
    grad_shift_one = jnp.sum(query_grad_low.astype(jnp.float32), axis=0)
    grad_shift_two = jnp.sum(value_grad_low.astype(jnp.float32), axis=0)
    grad_normed = times_transposed(grad_joined, back_qkv)
    grad_gain_one = jnp.sum(grad_normed * scaled_one, axis=0)
    grad_shift_zero = jnp.sum(grad_normed, axis=0)
    grad_inputs = grad_middle + norm_back(grad_normed, scaled_one, inverse_one, back_gains[0])
    grad_tokens = grad_inputs.astype(jnp.bfloat16).reshape(tokens.shape)
    grad_gains = jnp.stack([grad_gain_one, grad_gain_two])
    grad_shifts = jnp.stack(
        [
            grad_shift_zero,
            grad_shift_one,
            grad_shift_two,
            grad_shift_three,
            grad_shift_four,
            grad_shift_five,
        ]
    )
    shards = (
        lax.psum_scatter(
            grad_qkv.astype(jnp.bfloat16), "fsdp", scatter_dimension=0, tiled=True
        ).astype(jnp.float32),
        lax.psum_scatter(
            grad_out.astype(jnp.bfloat16), "fsdp", scatter_dimension=0, tiled=True
        ).astype(jnp.float32),
        lax.psum_scatter(
            grad_fc1.astype(jnp.bfloat16), "fsdp", scatter_dimension=0, tiled=True
        ).astype(jnp.float32),
        lax.psum_scatter(
            grad_fc2.astype(jnp.bfloat16), "fsdp", scatter_dimension=0, tiled=True
        ).astype(jnp.float32),
        lax.psum_scatter(
            grad_gains.astype(jnp.bfloat16), "fsdp", scatter_dimension=1, tiled=True
        ).astype(jnp.float32),
        lax.psum_scatter(
            grad_shifts.astype(jnp.bfloat16), "fsdp", scatter_dimension=1, tiled=True
        ).astype(jnp.float32),
        lax.psum_scatter(
            grad_hidden_shift.astype(jnp.bfloat16), "fsdp", scatter_dimension=0, tiled=True
        ).astype(jnp.float32),
    )
    summed = (
        lax.psum(shards[0].astype(jnp.bfloat16), ("rep", "seq")).astype(jnp.float32),
        lax.psum(shards[1].astype(jnp.bfloat16), ("rep", "seq")).astype(jnp.float32),
        lax.psum(shards[2].astype(jnp.bfloat16), ("rep", "seq")).astype(jnp.float32),
        lax.psum(shards[3].astype(jnp.bfloat16), ("rep", "seq")).astype(jnp.float32),
        lax.psum(shards[4].astype(jnp.bfloat16), ("rep", "seq")).astype(jnp.float32),
        lax.psum(shards[5].astype(jnp.bfloat16), ("rep", "seq")).astype(jnp.float32),
        lax.psum(shards[6].astype(jnp.bfloat16), ("rep", "seq")).astype(jnp.float32),
    )
    return (
        output,
        grad_tokens,
        summed[0],
        summed[1],
        summed[2],
        summed[3],
        summed[4],
        summed[5],
        summed[6],
    )


def solution(mesh):
    return jax.shard_map(
        on_device,
        mesh=mesh,
        in_specs=(
            P(("rep", "fsdp"), "seq", None),
            P(("rep", "fsdp")),
            P(("rep", "fsdp"), "seq", None),
            P("fsdp", None),
            P("fsdp", None),
            P("fsdp", None),
            P("fsdp", None),
            P(None, "fsdp"),
            P(None, "fsdp"),
            P("fsdp"),
        ),
        out_specs=(
            P(("rep", "fsdp"), "seq", None),
            P(("rep", "fsdp"), "seq", None),
            P("fsdp", None),
            P("fsdp", None),
            P("fsdp", None),
            P("fsdp", None),
            P(None, "fsdp"),
            P(None, "fsdp"),
            P("fsdp"),
        ),
        check_vma=False,
    )
```

profile of v0, /device:TPU:0, one launch (start us, length us, event | category | flops | bytes accessed | tf_op | source)
XLA Modules:
  0.0 1236.4 jit_solution(1024592312134364579)
XLA Ops:
  7.3 3.3 convert_element_type.215
  10.7 12.6 %all_gather.32 = bf16[2,1024]{1,0:T(2,128)(2,1)S(1)} all-gather(bf16[2,256]{1,0:T(2,128)(2,1)S(1)} %convert_element_type.210), channel_id=1, replica_groups=mesh['rep'=4,'fsdp'=4,'seq'=2] {'fsdp'}, dimensions={1}, use_global_device_ids=true | all-gather | bytes 5120 | tf_op jit(solution)/shard_map/all_gather | solution.py:113
  23.3 14.3 %all_gather.33 = bf16[6,1024]{1,0:T(8,128)(2,1)S(1)} all-gather(bf16[6,256]{1,0:T(8,128)(2,1)S(1)} %convert_element_type.212), channel_id=1, replica_groups=mesh['rep'=4,'fsdp'=4,'seq'=2] {'fsdp'}, dimensions={1}, use_global_device_ids=true | all-gather | bytes 15360 | tf_op jit(solution)/shard_map/all_gather | solution.py:114
  38.1 90.8 %all-gather.9.cloned.1.call-done = bf16[1024,3072]{1,0:T(8,128)(2,1)} async-done(((bf16[256,3072]{1,0:T(8,128)(2,1)}), bf16[1024,3072]{1,0:T(8,128)(2,1)}) %all-gather.9.cloned.1.call-update) | async-done | bytes 6291472 | tf_op jit(solution)/shard_map/all_gather | solution.py:109
  128.9 5.0 fusion.53
  136.8 2.9 fusion.36
  140.7 4.1 convert_element_type.224
  144.9 3.8 convert_element_type.228
  149.5 11.9 all_gather.39
  163.7 19.9 %all-gather.17.cloned.1.call-done = bf16[592,1024]{1,0:T(8,128)(2,1)} async-done(((bf16[296,1024]{1,0:T(8,128)(2,1)}), bf16[592,1024]{1,0:T(8,128)(2,1)}) %all-gather.17.cloned.1.call-update) | async-done | bytes 1212432 | tf_op jit(solution)/shard_map/all_gather | solution.py:145
  183.6 2.4 copy.31
  188.2 3.2 fusion
  193.1 4.5 fusion.20
  197.6 33.4 %all-gather.11.cloned.1.call-done = bf16[1024,1024]{1,0:T(8,128)(2,1)} async-done(((bf16[256,1024]{1,0:T(8,128)(2,1)}), bf16[1024,1024]{1,0:T(8,128)(2,1)}) %all-gather.11.cloned.1.call-update) | async-done | bytes 2097168 | tf_op jit(solution)/shard_map/all_gather | solution.py:110
  231.0 2.8 fusion.59
  234.1 147.3 %all-gather.13.cloned.1.call-done = bf16[1024,4096]{1,0:T(8,128)(2,1)} async-done(((bf16[256,4096]{1,0:T(8,128)(2,1)}), bf16[1024,4096]{1,0:T(8,128)(2,1)}) %all-gather.13.cloned.1.call-update) | async-done | bytes 8388624 | tf_op jit(solution)/shard_map/all_gather | solution.py:111
  381.4 8.5 convolution_add_fusion
  389.9 141.4 %all-gather.15.cloned.1.call-done = bf16[4096,1024]{1,0:T(8,128)(2,1)} async-done(((bf16[1024,1024]{1,0:T(8,128)(2,1)}), bf16[4096,1024]{1,0:T(8,128)(2,1)}) %all-gather.15.cloned.1.call-update) | async-done | bytes 8388624 | tf_op jit(solution)/shard_map/all_gather | solution.py:112
  531.3 9.1 fusion.61
  540.4 3.1 multiply_reduce_fusion.1
  549.0 8.5 fusion.9
  557.6 6.2 copy.37
  563.8 3.2 copy.46
  567.0 9.8 multiply_reduce_fusion
  576.8 6.6 multiply_convert_fusion
  583.4 2.9 convolution_convert_fusion.4
  586.4 6.2 copy.35
  592.6 3.1 copy.47
  595.8 4.1 convolution_convert_fusion.3
  600.4 5.6 fusion.60
  606.0 2.7 fusion.56
  610.9 5.2 reduce-scatter.25.cloned.1.call-done
  620.0 7.4 convolution_convert_fusion.2
  628.4 9.7 convolution_convert_fusion
  638.1 8.8 convolution_convert_fusion.1
  647.2 6.6 fusion.33
  655.7 7.2 reduce-scatter.17.cloned.1.call-done
  662.8 112.4 %reduce-scatter.15.cloned.1.call-done = bf16[256,3072]{1,0:T(8,128)(2,1)} async-done(((bf16[1024,3072]{1,0:T(8,128)(2,1)}), bf16[256,3072]{1,0:T(8,128)(2,1)}) %reduce-scatter.15.cloned.1.call-update) | async-done | bytes 1572880 | tf_op jit(solution)/shard_map/reduce_scatter | solution.py:236
  775.2 147.5 %reduce-scatter.21.cloned.1.call-done = bf16[1024,1024]{1,0:T(8,128)(2,1)} async-done(((bf16[4096,1024]{1,0:T(8,128)(2,1)}), bf16[1024,1024]{1,0:T(8,128)(2,1)}) %reduce-scatter.21.cloned.1.call-update) | async-done | bytes 2097168 | tf_op jit(solution)/shard_map/reduce_scatter | solution.py:245
  922.7 147.6 %reduce-scatter.19.cloned.1.call-done = bf16[256,4096]{1,0:T(8,128)(2,1)} async-done(((bf16[1024,4096]{1,0:T(8,128)(2,1)}), bf16[256,4096]{1,0:T(8,128)(2,1)}) %reduce-scatter.19.cloned.1.call-update) | async-done | bytes 2097168 | tf_op jit(solution)/shard_map/reduce_scatter | solution.py:242
  1072.1 11.4 all-reduce
  1083.6 8.6 fusion.25
  1094.5 18.9 %reduce-scatter.23.cloned.1.call-done = bf16[6,256]{1,0:T(8,128)(2,1)} async-done(((bf16[6,1024]{1,0:T(8,128)(2,1)}), bf16[6,256]{1,0:T(8,128)(2,1)}) %reduce-scatter.23.cloned.1.call-update) | async-done | bytes 3088 | tf_op jit(solution)/shard_map/reduce_scatter | solution.py:251
  1113.4 14.1 %all-reduce.1 = (bf16[2,256]{1,0:T(2,128)(2,1)S(1)}, bf16[6,256]{1,0:T(8,128)(2,1)S(1)}, bf16[1024]{0:T(1024)(128)(2,1)S(1)}) all-reduce(bf16[2,256]{1,0:T(2,128)(2,1)S(1)} %copy.40, bf16[6,256]{1,0:T(8,128)(2,1)} %reduce-scatter.23.cloned.1.call-done, ...), channel_id=1, replica_groups=mesh['rep'=4,'fsdp'=4,'seq'=2] {'rep','seq'}, use_global_device_ids=true, to_apply=%region_24.25 | all-reduce | flops 3072 | bytes 12288 | tf_op jit(solution)/shard_map/psum | solution.py:263
  1129.2 91.0 %all-reduce.5.cloned.1.call-done = (bf16[256,3072]{1,0:T(8,128)(2,1)}, bf16[256,1024]{1,0:T(8,128)(2,1)}, bf16[256,4096]{1,0:T(8,128)(2,1)}, bf16[1024,1024]{1,0:T(8,128)(2,1)}) async-done(((bf16[256,3072]{1,0:T(8,128)(2,1)}, bf16[256,1024]{1,0:T(8,128)(2,1)}, bf16[256,4096]{1,0:T(8,128)(2,1)}, bf16[1024,1024]{1,0:T(8,128)(2,1)}), (bf16[256,3072]{1,0:T(8,128)(2,1)}, bf16[256,1024]{1,0:T(8,128)(2,1)}, ...) | async-done | bytes 6291472 | tf_op jit(solution)/shard_map/psum | solution.py:259
  1220.3 2.2 convert_element_type.248
  1224.7 2.5 convert_element_type.250
  1227.2 2.5 convert_element_type.252
  (129 shorter events, 34.0 us)
Async XLA Ops:
  7.2 3.5 copy-start.19
  7.2 3.5 copy-start.17
  7.2 30.4 %copy-start.2 = (bf16[1,296,1024]{2,1,0:T(8,128)(2,1)S(1)}, bf16[1,296,1024]{2,1,0:T(8,128)(2,1)}, u32[]{:S(2)}) copy-start(bf16[1,296,1024]{2,1,0:T(8,128)(2,1)} %param.10) | copy-start | bytes 1818628
  7.2 121.7 %all-gather.9.cloned.1.call-start = ((), (), s32[]{:S(2)}) async-start(), calls=%async_computation.8 | async-start | bytes 7864320 | tf_op jit(solution)/shard_map/all_gather | solution.py:109
  10.6 151.2 %all-gather.19.cloned.1.call-start = ((), (), s32[]{:S(2)}) async-start(), calls=%async_computation.18 | async-start | bytes 1818624 | tf_op jit(solution)/shard_map/all_gather | solution.py:144
  134.0 1.8 copy-start.8
  136.7 46.9 %all-gather.17.cloned.1.call-start = ((), (), s32[]{:S(2)}) async-start(), calls=%async_computation.17 | async-start | bytes 1818624 | tf_op jit(solution)/shard_map/all_gather | solution.py:145
  136.8 3.0 copy-start.13
  139.7 91.3 %all-gather.11.cloned.1.call-start = ((), (), s32[]{:S(2)}) async-start(), calls=%async_computation.9 | async-start | bytes 2621440 | tf_op jit(solution)/shard_map/all_gather | solution.py:110
  140.7 240.7 %all-gather.13.cloned.1.call-start = ((), (), s32[]{:S(2)}) async-start(), calls=%async_computation.10 | async-start | bytes 10485760 | tf_op jit(solution)/shard_map/all_gather | solution.py:111
  144.8 386.4 %all-gather.15.cloned.1.call-start = ((), (), s32[]{:S(2)}) async-start(), calls=%async_computation.11 | async-start | bytes 10485760 | tf_op jit(solution)/shard_map/all_gather | solution.py:112
  148.7 0.7 copy-start.18
  148.7 457.3 %reduce-scatter.27.cloned.1.call-start = ((), (), s32[]{:S(2)}) async-start(), calls=%async_computation.20 | async-start | bytes 1818624
  161.7 24.3 %copy-start.5 = (bf16[296,1024]{0,1:T(8,128)(2,1)}, bf16[296,1024]{0,1:T(8,128)(2,1)S(1)}, u32[]{:S(2)}) copy-start(bf16[296,1024]{0,1:T(8,128)(2,1)S(1)} %copy.32) | copy-start | bytes 1818628
  188.2 4.9 copy-start
  188.2 4.9 copy-start.7
  531.3 9.1 copy-start.20
  540.3 3.1 copy-start.22
  540.3 3.1 copy-start.14
  543.5 1.6 copy-start.11
  544.1 1.0 copy-start.3
  567.0 49.1 %reduce-scatter.25.cloned.1.call-start = ((), (), s32[]{:S(2)}) async-start(), calls=%async_computation.19 | async-start | bytes 1818624
  576.8 6.6 copy-start.6
  583.4 3.0 copy-start.1
  595.8 67.0 %reduce-scatter.17.cloned.1.call-start = ((), (), s32[]{:S(2)}) async-start(), calls=%async_computation.13 | async-start | bytes 2621440 | tf_op jit(solution)/shard_map/reduce_scatter | solution.py:239
  600.0 175.2 %reduce-scatter.15.cloned.1.call-start = ((), (), s32[]{:S(2)}) async-start(), calls=%async_computation.12 | async-start | bytes 7864320 | tf_op jit(solution)/shard_map/reduce_scatter | solution.py:236
  627.3 1.1 copy-start.15
  627.4 295.3 %reduce-scatter.21.cloned.1.call-start = ((), (), s32[]{:S(2)}) async-start(), calls=%async_computation.15 | async-start | bytes 10485760 | tf_op jit(solution)/shard_map/reduce_scatter | solution.py:245
  638.1 432.1 %reduce-scatter.19.cloned.1.call-start = ((), (), s32[]{:S(2)}) async-start(), calls=%async_computation.14 | async-start | bytes 10485760 | tf_op jit(solution)/shard_map/reduce_scatter | solution.py:242
  647.0 446.6 %reduce-scatter.29.cloned.1.call-start = ((), (), s32[]{:S(2)}) async-start(), calls=%async_computation.21 | async-start | bytes 327680
  654.7 458.6 %reduce-scatter.23.cloned.1.call-start = ((), (), s32[]{:S(2)}) async-start(), calls=%async_computation.16 | async-start | bytes 20480 | tf_op jit(solution)/shard_map/reduce_scatter | solution.py:251
  655.6 564.7 %all-reduce.5.cloned.1.call-start = ((), (), s32[]{:S(2)}) async-start(), calls=%async_computation.22 | async-start | bytes 12582912 | tf_op jit(solution)/shard_map/psum | solution.py:259
  1070.2 0.7 copy-start.21
  1083.5 8.7 copy-start.16
  1083.5 8.7 copy-start.4
  1092.2 21.2 %dynamic-slice-start = ((bf16[4096]{0:T(1024)(128)(2,1)}, u32[]{:T(128)}), bf16[1024]{0:T(1024)(128)(2,1)S(1)}, s32[]{:S(2)}) async-start(bf16[4096]{0:T(1024)(128)(2,1)} %copy-done.16, u32[]{:T(128)} %multiply.49), calls=%async_computation.23 | async-start | bytes 4608
  1220.3 2.2 copy-start.12
  1222.5 2.2 copy-start.10
  1224.7 2.5 copy-start.9
Sparse Core Ops, SparseCore 0:
  10.7 118.1 all-gather.8
  136.8 21.4 all-gather.18
  160.4 23.1 all-gather.16
  185.0 45.9 all-gather.10
  233.0 148.3 all-gather.12
  383.4 147.8 all-gather.14
  567.1 20.3 reduce-scatter.26
  595.9 20.0 reduce-scatter.24
  618.9 43.8 reduce-scatter.16
  665.1 110.0 reduce-scatter.14
  777.6 144.9 reduce-scatter.20
  925.0 145.1 reduce-scatter.18
  1073.2 20.3 reduce-scatter.28
  1096.2 17.1 reduce-scatter.22
  1117.3 102.9 all-reduce.4
where the time goes:
time: 1240 us
  waiting for transfers between devices  963 us (78%)
  matrix products  109 us (9%)
  blocking collectives  64.3 us (5%)
  local copies, waits for them, and re-layouts  42.4 us (3%)
  other arithmetic  41.2 us (3%)
  between operations  15.9 us (1%)
    reduce_scatter x1, waiting for transfers between devices, on_device(): lax.psum_scatter(grad_fc1.astype(jnp.bfloat16), 'fsdp', scatter_dimension...  148 us
    reduce_scatter x1, waiting for transfers between devices, on_device(): lax.psum_scatter(grad_fc2.astype(jnp.bfloat16), 'fsdp', scatter_dimension...  148 us
    all_gather x1, waiting for transfers between devices, on_device(): lax.all_gather(low_fc1, 'fsdp', axis=0, tiled=True)  147 us
    all_gather x1, waiting for transfers between devices, on_device(): lax.all_gather(low_fc2, 'fsdp', axis=0, tiled=True)  141 us
    reduce_scatter x1, waiting for transfers between devices, on_device(): lax.psum_scatter(grad_qkv.astype(jnp.bfloat16), 'fsdp', scatter_dimension...  112 us
    psum x1, waiting for transfers between devices, on_device(): lax.psum(shards[0].astype(jnp.bfloat16), ('rep', 'seq')).astype(jnp.float32)  91 us
    all_gather x1, waiting for transfers between devices, on_device(): lax.all_gather(low_qkv, 'fsdp', axis=0, tiled=True)  90.8 us
    unnamed x58, local copies, waits for them, and re-layouts  33.7 us
  transfers between devices with their start and end apart: 15, of which 12 were waited for; matrix products, arithmetic and copies ran while one was open for 11% of the time, Pallas kernels for 0%

commit v1 on v0

--- a/solution.py
+++ b/solution.py
@@ -8,6 +8,18 @@
 IMG_TOK = 577
 EPSILON = 1e-05
 NEGATIVE = -1e30
+
+
+def gather_around(shard, axis, dim):
+    ways, here, step = (lax.axis_size(axis), lax.axis_index(axis), shard.shape[dim])
+    lengths = [n * ways if d == dim else n for d, n in enumerate(shard.shape)]
+    full = lax.dynamic_update_slice_in_dim(
+        jnp.zeros(lengths, shard.dtype), shard, here * step, axis=dim
+    )
+    for far in range(1, ways):
+        shard = lax.ppermute(shard, axis, [(d, (d + 1) % ways) for d in range(ways)])
+        full = lax.dynamic_update_slice_in_dim(full, shard, (here - far) % ways * step, axis=dim)
+    return full
 
 
 def normalize(inputs, gain_row, shift_row):
@@ -109,7 +121,7 @@
         lax.all_gather(low_qkv, "fsdp", axis=0, tiled=True),
         lax.all_gather(low_out, "fsdp", axis=0, tiled=True),
         lax.all_gather(low_fc1, "fsdp", axis=0, tiled=True),
-        lax.all_gather(low_fc2, "fsdp", axis=0, tiled=True),
+        gather_around(low_fc2, "fsdp", 0),
         lax.all_gather(low_gains, "fsdp", axis=1, tiled=True),
         lax.all_gather(low_biases, "fsdp", axis=1, tiled=True),
         lax.all_gather(low_fc1_bias, "fsdp", axis=0, tiled=True),

time: 1240 us -> 1360 us (1.097)
  waiting for transfers between devices: 963 us -> 1040 us
  starting transfers between devices: 1.2 us -> 23.5 us
  local copies, waits for them, and re-layouts: 42.4 us -> 58.1 us
    ppermute x0 -> x3, waiting for transfers between devices: none -> 176 us  [gather_around(): lax.ppermute(shard, axis, [(d, (d + 1) % ways) for d in range(ways)])]
    reduce_scatter x1, waiting for transfers between devices: 112 us -> 2.37 us  [on_device(): lax.psum_scatter(grad_qkv.astype(jnp.bfloat16), 'fsdp', scatter_dimension...]
    reduce_scatter x1, waiting for transfers between devices: 148 us -> 177 us  [on_device(): lax.psum_scatter(grad_fc1.astype(jnp.bfloat16), 'fsdp', scatter_dimension...]
    ppermute x0 -> x3, starting transfers between devices: none -> 22.5 us  [gather_around(): lax.ppermute(shard, axis, [(d, (d + 1) % ways) for d in range(ways)])]
    all_gather x1, waiting for transfers between devices: 19.9 us -> 0.02 us  [on_device(): lax.all_gather(values_local, 'seq', axis=1, tiled=True)]
    all_gather x1, waiting for transfers between devices: 0.02 us -> 16.7 us  [on_device(): lax.all_gather(keys_local, 'seq', axis=1, tiled=True)]
    unnamed x58 -> x62, local copies, waits for them, and re-layouts: 33.7 us -> 34.6 us
  transfers between devices with their start and end apart: 15 -> 18, of which waited for: 12 -> 13; matrix products, arithmetic and copies ran while one was open for 11% -> 11% of each run, Pallas kernels for 0% -> 0%
where the time goes in v1:
time: 1360 us; the launch traced here: 1350 us
  waiting for transfers between devices  1040 us (76%)
  matrix products  109 us (8%)
  blocking collectives  64.6 us (5%)
  local copies, waits for them, and re-layouts  58.1 us (4%)
  other arithmetic  38.7 us (3%)
  starting transfers between devices  23.5 us (2%)
  between operations  16 us (1%)
    reduce_scatter x1, waiting for transfers between devices, on_device(): lax.psum_scatter(grad_fc1.astype(jnp.bfloat16), 'fsdp', scatter_dimension...  177 us
    ppermute x3, waiting for transfers between devices, gather_around(): lax.ppermute(shard, axis, [(d, (d + 1) % ways) for d in range(ways)])  176 us
    all_gather x1, waiting for transfers between devices, on_device(): lax.all_gather(low_fc1, 'fsdp', axis=0, tiled=True)  147 us
    reduce_scatter x1, waiting for transfers between devices, on_device(): lax.psum_scatter(grad_fc2.astype(jnp.bfloat16), 'fsdp', scatter_dimension...  146 us
    all_gather x1, waiting for transfers between devices, on_device(): lax.all_gather(low_fc2, 'fsdp', axis=0, tiled=True)  141 us
    psum x1, waiting for transfers between devices, on_device(): lax.psum(shards[0].astype(jnp.bfloat16), ('rep', 'seq')).astype(jnp.float32)  91.1 us
    all_gather x1, waiting for transfers between devices, on_device(): lax.all_gather(low_qkv, 'fsdp', axis=0, tiled=True)  90.8 us
    all_gather x1, waiting for transfers between devices, on_device(): lax.all_gather(low_out, 'fsdp', axis=0, tiled=True)  34.9 us
  transfers between devices with their start and end apart: 18, of which 13 were waited for; matrix products, arithmetic and copies ran while one was open for 11% of the time, Pallas kernels for 0%

profile of v1, /device:TPU:0, one launch (start us, length us, event | category | flops | bytes accessed | tf_op | source)
XLA Modules:
  0.0 1347.9 jit_solution(11977238436621204758)
XLA Ops:
  7.3 3.3 convert_element_type.215
  10.7 12.6 all_gather.31
  23.3 14.3 %all_gather.32 = bf16[6,1024]{1,0:T(8,128)(2,1)S(1)} all-gather(bf16[6,256]{1,0:T(8,128)(2,1)S(1)} %convert_element_type.212), channel_id=1, replica_groups=mesh['rep'=4,'fsdp'=4,'seq'=2] {'fsdp'}, dimensions={1}, use_global_device_ids=true | all-gather | bytes 15360 | tf_op jit(solution)/shard_map/all_gather | solution.py:126
  38.1 90.8 %all-gather.9.cloned.1.call-done = bf16[1024,3072]{1,0:T(8,128)(2,1)} async-done(((bf16[256,3072]{1,0:T(8,128)(2,1)}), bf16[1024,3072]{1,0:T(8,128)(2,1)}) %all-gather.9.cloned.1.call-update) | async-done | bytes 6291472 | tf_op jit(solution)/shard_map/all_gather | solution.py:121
  128.9 5.0 fusion.53
  140.2 4.1 convert_element_type.224
  144.4 4.3 broadcast_in_dim.64
  152.2 11.9 all_gather.38
  167.2 16.7 %all-gather.19.cloned.1.call-done = bf16[592,1024]{1,0:T(8,128)(2,1)} async-done(((bf16[296,1024]{1,0:T(8,128)(2,1)}), bf16[592,1024]{1,0:T(8,128)(2,1)}) %all-gather.19.cloned.1.call-update) | async-done | bytes 1212432 | tf_op jit(solution)/shard_map/all_gather | solution.py:156
  187.8 3.2 fusion
  192.4 4.5 fusion.20
  197.0 34.9 %all-gather.11.cloned.1.call-done = bf16[1024,1024]{1,0:T(8,128)(2,1)} async-done(((bf16[256,1024]{1,0:T(8,128)(2,1)}), bf16[1024,1024]{1,0:T(8,128)(2,1)}) %all-gather.11.cloned.1.call-update) | async-done | bytes 2097168 | tf_op jit(solution)/shard_map/all_gather | solution.py:122
  231.9 2.8 fusion.59
  235.0 147.2 %all-gather.13.cloned.1.call-done = bf16[1024,4096]{1,0:T(8,128)(2,1)} async-done(((bf16[256,4096]{1,0:T(8,128)(2,1)}), bf16[1024,4096]{1,0:T(8,128)(2,1)}) %all-gather.13.cloned.1.call-update) | async-done | bytes 8388624 | tf_op jit(solution)/shard_map/all_gather | solution.py:123
  382.2 8.5 convolution_add_fusion
  390.7 141.4 %all-gather.15.cloned.1.call-done = bf16[4096,1024]{1,0:T(8,128)(2,1)} async-done(((bf16[1024,1024]{1,0:T(8,128)(2,1)}), bf16[4096,1024]{1,0:T(8,128)(2,1)}) %all-gather.15.cloned.1.call-update) | async-done | bytes 8388624 | tf_op jit(solution)/shard_map/all_gather | solution.py:175
  532.1 9.1 fusion.61
  541.2 3.1 multiply_reduce_fusion.1
  549.8 8.5 fusion.9
  558.4 6.2 copy.37
  564.6 3.2 copy.46
  567.8 9.8 multiply_reduce_fusion
  577.6 6.6 multiply_convert_fusion
  584.2 2.9 convolution_convert_fusion.4
  587.2 6.2 copy.35
  593.4 3.2 copy.47
  596.7 4.1 convolution_convert_fusion.3
  601.2 5.5 fusion.60
  611.6 5.2 reduce-scatter.25.cloned.1.call-done
  620.8 7.4 convolution_convert_fusion.2
  628.3 8.8 convolution_convert_fusion.1
  638.1 9.6 convolution_convert_fusion
  649.3 81.1 %collective-permute-done = bf16[1024,1024]{1,0:T(8,128)(2,1)S(1)} collective-permute-done((bf16[1024,1024]{1,0:T(8,128)(2,1)}, bf16[1024,1024]{1,0:T(8,128)(2,1)S(1)}, u32[]{:S(2)}, u32[]{:S(2)}) %collective-permute-start) | collective-permute-done | bytes 2097184 | tf_op jit(solution)/shard_map/ppermute | solution.py:20
  731.7 17.3 %collective-permute-start.1 = (bf16[1024,1024]{1,0:T(8,128)(2,1)S(1)}, bf16[1024,1024]{1,0:T(8,128)(2,1)}, u32[]{:S(2)}, u32[]{:S(2)}) collective-permute-start(bf16[1024,1024]{1,0:T(8,128)(2,1)S(1)} %collective-permute-done), channel_id=1, source_target_pairs={{0,2},{2,4},{4,6},{6,0},{1,3},{3,5},{5,7},{7,1},{8,10},{10,12},{12... | collective-permute-start | bytes 6291464 | tf_op jit(solution)/shard_map/ppermute | solution.py:20
  749.0 94.7 %collective-permute-done.1 = bf16[1024,1024]{1,0:T(8,128)(2,1)} collective-permute-done((bf16[1024,1024]{1,0:T(8,128)(2,1)S(1)}, bf16[1024,1024]{1,0:T(8,128)(2,1)}, u32[]{:S(2)}, u32[]{:S(2)}) %collective-permute-start.1) | collective-permute-done | bytes 2097184 | tf_op jit(solution)/shard_map/ppermute | solution.py:20
  843.8 3.6 collective-permute-start.2
  847.3 6.5 fusion.33
  858.1 177.2 %reduce-scatter.19.cloned.1.call-done = bf16[256,4096]{1,0:T(8,128)(2,1)} async-done(((bf16[1024,4096]{1,0:T(8,128)(2,1)}), bf16[256,4096]{1,0:T(8,128)(2,1)}) %reduce-scatter.19.cloned.1.call-update) | async-done | bytes 2097168 | tf_op jit(solution)/shard_map/reduce_scatter | solution.py:254
  1035.4 145.7 %reduce-scatter.21.cloned.1.call-done = bf16[1024,1024]{1,0:T(8,128)(2,1)} async-done(((bf16[4096,1024]{1,0:T(8,128)(2,1)}), bf16[1024,1024]{1,0:T(8,128)(2,1)}) %reduce-scatter.21.cloned.1.call-update) | async-done | bytes 2097168 | tf_op jit(solution)/shard_map/reduce_scatter | solution.py:257
  1183.0 3.1 constant_dynamic-update-slice_fusion.2
  1186.0 3.1 constant_dynamic-update-slice_fusion.1
  1189.1 3.1 constant_dynamic-update-slice_fusion
  1192.2 11.7 all-reduce
  1204.0 8.6 fusion.25
  1214.8 9.7 reduce-scatter.23.cloned.1.call-done
  1224.5 14.1 %all-reduce.1 = (bf16[2,256]{1,0:T(2,128)(2,1)S(1)}, bf16[6,256]{1,0:T(8,128)(2,1)S(1)}, bf16[1024]{0:T(1024)(128)(2,1)S(1)}) all-reduce(bf16[2,256]{1,0:T(2,128)(2,1)S(1)} %copy.40, bf16[6,256]{1,0:T(8,128)(2,1)} %reduce-scatter.23.cloned.1.call-done, ...), channel_id=1, replica_groups=mesh['rep'=4,'fsdp'=4,'seq'=2] {'rep','seq'}, use_global_device_ids=true, to_apply=%region_24.25 | all-reduce | flops 3072 | bytes 12288 | tf_op jit(solution)/shard_map/psum | solution.py:275
  1240.4 91.1 %all-reduce.5.cloned.1.call-done = (bf16[256,3072]{1,0:T(8,128)(2,1)}, bf16[256,1024]{1,0:T(8,128)(2,1)}, bf16[256,4096]{1,0:T(8,128)(2,1)}, bf16[1024,1024]{1,0:T(8,128)(2,1)}) async-done(((bf16[256,3072]{1,0:T(8,128)(2,1)}, bf16[256,1024]{1,0:T(8,128)(2,1)}, bf16[256,4096]{1,0:T(8,128)(2,1)}, bf16[1024,1024]{1,0:T(8,128)(2,1)}), (bf16[256,3072]{1,0:T(8,128)(2,1)}, bf16[256,1024]{1,0:T(8,128)(2,1)}, ...) | async-done | bytes 6291472 | tf_op jit(solution)/shard_map/psum | solution.py:271
  1331.5 3.6 convert_element_type.246
  (143 shorter events, 52.9 us)
Async XLA Ops:
  7.2 3.5 copy-start.19
  7.2 3.5 copy-start.21
  7.2 30.4 %copy-start.2 = (bf16[1,296,1024]{2,1,0:T(8,128)(2,1)S(1)}, bf16[1,296,1024]{2,1,0:T(8,128)(2,1)}, u32[]{:S(2)}) copy-start(bf16[1,296,1024]{2,1,0:T(8,128)(2,1)} %param.10) | copy-start | bytes 1818628
  7.2 121.7 %all-gather.9.cloned.1.call-start = ((), (), s32[]{:S(2)}) async-start(), calls=%async_computation.8 | async-start | bytes 7864320 | tf_op jit(solution)/shard_map/all_gather | solution.py:121
  10.6 153.9 %all-gather.17.cloned.1.call-start = ((), (), s32[]{:S(2)}) async-start(), calls=%async_computation.17 | async-start | bytes 1818624 | tf_op jit(solution)/shard_map/all_gather | solution.py:157
  134.0 1.8 copy-start.9
  135.8 3.5 copy-start.14
  137.0 46.9 %all-gather.19.cloned.1.call-start = ((), (), s32[]{:S(2)}) async-start(), calls=%async_computation.18 | async-start | bytes 1818624 | tf_op jit(solution)/shard_map/all_gather | solution.py:156
  139.2 92.6 %all-gather.11.cloned.1.call-start = ((), (), s32[]{:S(2)}) async-start(), calls=%async_computation.9 | async-start | bytes 2621440 | tf_op jit(solution)/shard_map/all_gather | solution.py:122
  140.2 242.0 %all-gather.13.cloned.1.call-start = ((), (), s32[]{:S(2)}) async-start(), calls=%async_computation.10 | async-start | bytes 10485760 | tf_op jit(solution)/shard_map/all_gather | solution.py:123
  144.3 387.7 %all-gather.15.cloned.1.call-start = ((), (), s32[]{:S(2)}) async-start(), calls=%async_computation.11 | async-start | bytes 10485760 | tf_op jit(solution)/shard_map/all_gather | solution.py:175
  144.4 4.4 copy-start.8
  148.7 3.4 copy-start.20
  151.5 455.3 %reduce-scatter.27.cloned.1.call-start = ((), (), s32[]{:S(2)}) async-start(), calls=%async_computation.20 | async-start | bytes 1818624
  164.4 21.1 %copy-start.5 = (bf16[296,1024]{0,1:T(8,128)(2,1)}, bf16[296,1024]{0,1:T(8,128)(2,1)S(1)}, u32[]{:S(2)}) copy-start(bf16[296,1024]{0,1:T(8,128)(2,1)S(1)} %copy.32) | copy-start | bytes 1818628
  187.8 4.7 copy-start
  187.8 4.7 copy-start.7
  532.1 9.1 copy-start.22
  541.1 3.1 copy-start.24
  541.2 3.1 copy-start.15
  544.3 1.7 copy-start.13
  544.9 1.1 copy-start.3
  567.8 49.1 %reduce-scatter.25.cloned.1.call-start = ((), (), s32[]{:S(2)}) async-start(), calls=%async_computation.19 | async-start | bytes 1818624
  577.6 6.6 copy-start.6
  584.2 3.0 copy-start.1
  596.6 259.2 %reduce-scatter.17.cloned.1.call-start = ((), (), s32[]{:S(2)}) async-start(), calls=%async_computation.13 | async-start | bytes 2621440 | tf_op jit(solution)/shard_map/reduce_scatter | solution.py:251
  600.8 257.4 %reduce-scatter.15.cloned.1.call-start = ((), (), s32[]{:S(2)}) async-start(), calls=%async_computation.12 | async-start | bytes 7864320 | tf_op jit(solution)/shard_map/reduce_scatter | solution.py:248
  628.2 407.1 %reduce-scatter.19.cloned.1.call-start = ((), (), s32[]{:S(2)}) async-start(), calls=%async_computation.14 | async-start | bytes 10485760 | tf_op jit(solution)/shard_map/reduce_scatter | solution.py:254
  637.1 1.1 copy-start.16
  637.1 544.0 %reduce-scatter.21.cloned.1.call-start = ((), (), s32[]{:S(2)}) async-start(), calls=%async_computation.15 | async-start | bytes 10485760 | tf_op jit(solution)/shard_map/reduce_scatter | solution.py:257
  647.7 566.2 %reduce-scatter.29.cloned.1.call-start = ((), (), s32[]{:S(2)}) async-start(), calls=%async_computation.21 | async-start | bytes 327680
  647.8 82.7 %collective-permute-start = (bf16[1024,1024]{1,0:T(8,128)(2,1)}, bf16[1024,1024]{1,0:T(8,128)(2,1)S(1)}, u32[]{:S(2)}, u32[]{:S(2)}) collective-permute-start(bf16[1024,1024]{1,0:T(8,128)(2,1)} %get-tuple-element.74), channel_id=1, source_target_pairs={{0,2},{2,4},{4,6},{6,0},{1,3},{3,5},{5,7},{7,1},{8,10},{10,12},{12... | collective-permute-start | bytes 6291464 | tf_op jit(solution)/shard_map/ppermute | solution.py:20
  730.4 1.3 copy-start.12
  731.7 112.0 %collective-permute-start.1 = (bf16[1024,1024]{1,0:T(8,128)(2,1)S(1)}, bf16[1024,1024]{1,0:T(8,128)(2,1)}, u32[]{:S(2)}, u32[]{:S(2)}) collective-permute-start(bf16[1024,1024]{1,0:T(8,128)(2,1)S(1)} %collective-permute-done), channel_id=1, source_target_pairs={{0,2},{2,4},{4,6},{6,0},{1,3},{3,5},{5,7},{7,1},{8,10},{10,12},{12... | collective-permute-start | bytes 6291464 | tf_op jit(solution)/shard_map/ppermute | solution.py:20
  843.8 345.3 %collective-permute-start.2 = (bf16[1024,1024]{1,0:T(8,128)(2,1)}, bf16[1024,1024]{1,0:T(8,128)(2,1)}, u32[]{:S(2)}, u32[]{:S(2)}) collective-permute-start(bf16[1024,1024]{1,0:T(8,128)(2,1)} %collective-permute-done.1), channel_id=1, source_target_pairs={{0,2},{2,4},{4,6},{6,0},{1,3},{3,5},{5,7},{7,1},{8,10},{10,12},{12... | collective-permute-start | bytes 6291464 | tf_op jit(solution)/shard_map/ppermute | solution.py:20
  854.8 369.7 %reduce-scatter.23.cloned.1.call-start = ((), (), s32[]{:S(2)}) async-start(), calls=%async_computation.16 | async-start | bytes 20480 | tf_op jit(solution)/shard_map/reduce_scatter | solution.py:263
  855.7 475.8 %all-reduce.5.cloned.1.call-start = ((), (), s32[]{:S(2)}) async-start(), calls=%async_computation.22 | async-start | bytes 12582912 | tf_op jit(solution)/shard_map/psum | solution.py:271
  1181.1 0.7 copy-start.23
  1203.9 8.7 copy-start.18
  1204.0 8.7 copy-start.4
  1212.6 12.0 dynamic-slice-start
  1331.5 3.6 copy-start.17
  1331.5 4.7 copy-start.11
  1336.2 2.5 copy-start.10
Sparse Core Ops, SparseCore 0:
  10.7 118.1 all-gather.8
  137.1 21.4 all-gather.16
  160.7 23.1 all-gather.18
  185.8 45.9 all-gather.10
  233.9 148.2 all-gather.12
  384.2 147.8 all-gather.14
  567.9 20.3 reduce-scatter.26
  596.7 20.0 reduce-scatter.24
  619.1 52.8 reduce-scatter.16
  674.3 183.8 reduce-scatter.14
  860.6 174.6 reduce-scatter.18
  1037.7 143.3 reduce-scatter.20
  1184.0 20.7 reduce-scatter.28
  1207.4 17.0 reduce-scatter.22
  1228.4 103.0 all-reduce.4
